TPU v7x, 32 devices: a whole 2x2x4 slice. The times are simulated.
32 devices in a mesh: groups: 2 (over x), sect: 8 (over z, y), head: 2 (over core).
Axes of the slice: x: 2, y: 2, z: 4, core: 2. Of those that a mesh axis runs over, the one named last changes fastest.
Arguments:
- queries: bfloat16 [2048, 8192], P(('groups', 'sect'), 'head'), parts along dimension 0, may hold values from -200 to 200
- packed_key_rows: bfloat16 [2048, 512], P(('groups', 'sect'), 'head'), parts along dimension 0, may hold values from -7 to 7
- values: bfloat16 [2048, 512], P(('groups', 'sect'), 'head'), parts along dimension 0, may hold values from -12 to 12
- segments: int32 [2048], P('groups'), parts along dimension 0, may hold values from 0 to 7, never falling along the last dimension, each value on 1 to 512 neighbouring positions
- proj_weight: bfloat16 [8192, 2048], P('head', 'sect'), may hold values from -0.0625 to 0.0625
- residual: bfloat16 [2048, 2048], P(('groups', 'sect', 'head')), parts along dimension 0, may hold values from -2 to 2
- norm_gain: bfloat16 [2048], replicated, may hold values from 0.5 to 1.5
- expert_ids: int32 [2048, 8], P(('groups', 'sect', 'head')), parts along dimension 0, may hold values from 0 to 15, all different within a row; in each aligned block of 64 rows (0 to 63, 64 to 127, ...) at most 48 rows name the same one
- route_weights: float32 [2048, 8], P(('groups', 'sect', 'head')), parts along dimension 0, may hold values from 0.05 to 1
- gate_weight: bfloat16 [16, 2048, 768], P(('sect', 'head')), may hold values from -0.125 to 0.125
- up_weight: bfloat16 [16, 2048, 768], P(('sect', 'head')), may hold values from -0.125 to 0.125
- down_weight: bfloat16 [16, 768, 2048], P(('sect', 'head')), may hold values from -0.21875 to 0.21875
Outputs:
- hidden_mid: bfloat16 [2048, 2048], P(('groups', 'sect', 'head')), parts along dimension 0
- expert_mix: bfloat16 [2048, 2048], P(('groups', 'sect', 'head')), parts along dimension 0
There are 2 independent parts, one for each index of `groups`. A program takes and returns all parts, laid end to end along the dimension named above; an argument that names none is the same for every part. Nothing has to cross between parts.
Inputs may be any that keep to these rules, and one draw needn't show every extreme that they name: `segments`: ids never fall along the rows; each of the 8 prompts has 1 to 512 rows, and one has exactly that many. `expert_ids`: each row names 8 different experts. Within the rows of one device (aligned blocks of 64 rows) no expert is named by more than 48 rows.
All inputs are finite; a program needn't handle non-finite values.
Results may differ from a plain program's by a relative error of at most 0.02.
Values may be sent and summed in bfloat16 or wider, within the bound.
A program may use at most 256 MiB of HBM per device.

v0:
```python
import math
import jax
import jax.numpy as jnp
from jax import lax
from jax.sharding import PartitionSpec as P

HEAD_WIDTH = 128
negative_large = -1e30
norm_eps = 1e-06


def attend(query_groups, packed_key_rows, values, segments, head_size):
    kv_heads = packed_key_rows.shape[1] // head_size
    score_scale = 1.0 / math.sqrt(head_size)
    prepared = []
    initial_state = []
    for query_rows, query_pos in query_groups:
        query_count = query_rows.shape[0]
        query_group_width = query_rows.shape[1] // head_size // kv_heads
        query_tensor_four = query_rows.reshape(query_count, kv_heads, query_group_width, head_size)
        query_seg = jnp.take(segments, query_pos)
        seg_start = jnp.sum((segments[None, :] < query_seg[:, None]).astype(jnp.int32), axis=1)
        prepared.append(
            (query_tensor_four, query_pos, query_seg, jnp.min(seg_start), jnp.max(query_pos))
        )
        initial_state.append(
            (
                jnp.full((query_count, kv_heads, query_group_width), negative_large, jnp.float32),
                jnp.zeros((query_count, kv_heads, query_group_width), jnp.float32),
                jnp.zeros((query_count, kv_heads, query_group_width, head_size), jnp.float32),
            )
        )
    running = tuple(initial_state)
    first_row = jnp.int32(0)
    key_piece = lax.all_gather(packed_key_rows, "sect", axis=0, tiled=True)
    value_piece = lax.all_gather(values, "sect", axis=0, tiled=True)
    piece_len = key_piece.shape[0]
    key_tensor_three = key_piece.reshape(piece_len, kv_heads, head_size)
    value_tensor_three = value_piece.reshape(piece_len, kv_heads, head_size)
    key_pos = jnp.arange(piece_len, dtype=jnp.int32)
    updated = []
    for state, setup in zip(running, prepared):
        query_tensor_four, query_pos, query_seg, lowest, highest = setup
        needed = jnp.logical_and(first_row <= highest, first_row + piece_len - 1 >= lowest)

        def compute(
            current, query_tensor_four=query_tensor_four, query_pos=query_pos, query_seg=query_seg
        ):
            run_max, run_sum, run_acc = current
            scores = (
                jnp.einsum(
                    "rkgd,pkd->rkgp",
                    query_tensor_four,
                    key_tensor_three,
                    preferred_element_type=jnp.float32,
                )
                * score_scale
            )
            allowed = jnp.logical_and(
                segments[None, :] == query_seg[:, None], key_pos[None, :] <= query_pos[:, None]
            )
            allowed = allowed[:, None, None, :]
            block_max = jnp.max(jnp.where(allowed, scores, negative_large), axis=-1)
            new_max = jnp.maximum(run_max, block_max)
            weights = jnp.where(allowed, jnp.exp(scores - new_max[..., None]), 0.0).astype(
                jnp.bfloat16
            )
            new_sum = jnp.sum(weights.astype(jnp.float32), axis=-1)
            new_acc = jnp.einsum(
                "rkgp,pkd->rkgd", weights, value_tensor_three, preferred_element_type=jnp.float32
            )
            return (new_max, new_sum, new_acc)

        updated.append(lax.cond(needed, compute, lambda kept: kept, state))
    final_state = tuple(updated)
    results = []
    for run_max, run_sum, run_acc in final_state:
        attended = run_acc / run_sum[..., None]
        results.append(attended.reshape(attended.shape[0], -1).astype(jnp.bfloat16))
    return results


def shards(
    queries,
    packed_key_rows,
    values,
    segments,
    proj_weight,
    residual,
    norm_gain,
    expert_ids,
    route_weights,
    gate_weight,
    up_weight,
    down_weight,
):
    row_count = queries.shape[0]
    sect_count = lax.axis_size("sect")
    head_count = lax.axis_size("head")
    sect_pos = lax.axis_index("sect")
    local_pos = jnp.arange(row_count, dtype=jnp.int32)
    own_pos = sect_pos * row_count + local_pos
    attended = attend([(queries, own_pos)], packed_key_rows, values, segments, HEAD_WIDTH)[0]
    partial_value = jnp.dot(
        attended,
        lax.all_gather(proj_weight, "sect", axis=1, tiled=True),
        preferred_element_type=jnp.float32,
    )
    projected = lax.psum_scatter(
        partial_value.astype(jnp.bfloat16), "head", scatter_dimension=0, tiled=True
    ).astype(jnp.float32)
    hidden_mid = (residual.astype(jnp.float32) + projected).astype(jnp.bfloat16)
    mid_float = lax.optimization_barrier(hidden_mid).astype(jnp.float32)
    inverse = lax.rsqrt(jnp.mean(mid_float * mid_float, axis=1, keepdims=True) + norm_eps)
    normed = (mid_float * inverse * norm_gain.astype(jnp.float32)[None, :]).astype(jnp.bfloat16)
    moe_rows = residual.shape[0]
    top_count = expert_ids.shape[1]
    experts = sect_count * head_count
    capacity = max(2, 3 * moe_rows * top_count // (2 * experts))
    flat_ids = expert_ids.reshape(-1)
    onehot = (flat_ids[:, None] == jnp.arange(experts, dtype=jnp.int32)[None, :]).astype(jnp.int32)
    slot_rank = jnp.sum((jnp.cumsum(onehot, axis=0) - 1) * onehot, axis=1)
    slot_index = flat_ids * capacity + slot_rank
    sources = jnp.repeat(normed, top_count, axis=0)
    outgoing = (
        jnp.zeros((experts * capacity, normed.shape[1]), jnp.bfloat16).at[slot_index].set(sources)
    )
    parcels = outgoing.reshape(experts, capacity, -1)
    slot_rows = lax.all_to_all(parcels, ("sect", "head"), split_axis=0, concat_axis=0, tiled=True)
    flat_rows = slot_rows.reshape(-1, slot_rows.shape[-1])
    gate_act = jnp.dot(flat_rows, gate_weight[0], preferred_element_type=jnp.float32)
    up_act = jnp.dot(flat_rows, up_weight[0], preferred_element_type=jnp.float32)
    hidden = (jax.nn.silu(gate_act) * up_act).astype(jnp.bfloat16)
    result = jnp.dot(hidden, down_weight[0], preferred_element_type=jnp.float32).astype(
        jnp.bfloat16
    )
    processed = result.reshape(slot_rows.shape)
    returned_rows = lax.all_to_all(
        processed, ("sect", "head"), split_axis=0, concat_axis=0, tiled=True
    )
    returned_flat = returned_rows.reshape(experts * capacity, -1)
    gathered = returned_flat[slot_index].reshape(moe_rows, top_count, -1)
    route_share = route_weights / jnp.sum(route_weights, axis=1, keepdims=True)
    mixture = jnp.sum(route_share[:, :, None] * gathered.astype(jnp.float32), axis=1)
    return (hidden_mid, mixture.astype(jnp.bfloat16))


def solution(mesh):
    placed = (
        P(("groups", "sect"), "head"),
        P(("groups", "sect"), "head"),
        P(("groups", "sect"), "head"),
        P("groups"),
        P("head", "sect"),
        P(("groups", "sect", "head"), None),
        P(),
        P(("groups", "sect", "head"), None),
        P(("groups", "sect", "head"), None),
        P(("sect", "head"), None, None),
        P(("sect", "head"), None, None),
        P(("sect", "head"), None, None),
    )
    return jax.shard_map(
        shards,
        mesh=mesh,
        in_specs=placed,
        out_specs=(P(("groups", "sect", "head"), None), P(("groups", "sect", "head"), None)),
        check_vma=False,
    )
```

profile of v0, /device:TPU:13, one launch (start us, length us, event | category | flops | bytes accessed | tf_op | source)
XLA Modules:
  0.0 462.3 jit_solution(15963046055641040890)
XLA Ops:
  7.2 0.0 copy-start
  7.2 0.0 copy-start.1
  7.2 0.0 all-gather.2.cloned.1.call-start
  7.2 0.7 all-gather.2.cloned.1.call-update
  7.9 0.0 reduce-scatter.2.cloned.1.call-start
  8.0 1.8 gather_fusion
  9.8 0.6 and_select_fusion.1
  11.1 0.9 convert_reduce_fusion.1
  12.0 0.6 reduce_min.9
  13.3 32.1 %all_gather.9 = bf16[1024,256]{1,0:T(8,128)(2,1)} all-gather(bf16[128,256]{1,0:T(8,128)(2,1)} %param.15), channel_id=1, replica_groups=mesh['groups'=2,'sect'=8,'head'=2] {'sect'}, dimensions={0}, use_global_device_ids=true | all-gather | bytes 589824 | tf_op jit(solution)/shard_map/all_gather | solution.py:35
  45.4 0.0 copy-done.4
  45.4 33.5 %all_gather.10 = bf16[1024,256]{1,0:T(8,128)(2,1)} all-gather(bf16[128,256]{1,0:T(8,128)(2,1)S(1)} %copy-done.4), channel_id=1, replica_groups=mesh['groups'=2,'sect'=8,'head'=2] {'sect'}, dimensions={0}, use_global_device_ids=true | all-gather | bytes 589824 | tf_op jit(solution)/shard_map/all_gather | solution.py:36
  78.9 40.8 %conditional.1 = (f32[128,2,16]{0,2,1:T(8,128)S(1)}, f32[128,2,16,128]{0,3,2,1:T(8,128)}) conditional(s32[]{:T(128)} %convert_element_type.61, () %tuple.16, (s32[1024]{0:T(1024)S(1)}, s32[128]{0:T(128)S(1)}, s32[128]{0:T(128)S(1)}, s32[128]{0:T(128)S(1)}, s32[1024]{0:T(1024)S(1)}, /*index=5*/s32[128]{0:T(128)S(1)}, bf16[1024,256]{1,0:T(8,128)(2,1)}, ...), branch_computations={%region_3.4_spmd, %region_4.0_spmd} | conditional | flops 2202399232 | bytes 63548432 | solution.py:74
  78.9 0.3 compare_and_fusion
  79.2 2.4 copy.61
  81.7 2.0 reshape.167
  83.6 9.8 %fusion = (f32[128,2,16]{0,2,1:T(8,128)S(1)}, f32[2,1024,128,16]{2,1,3,0:T(8,128)}) fusion(pred[128,1024]{0,1:T(8,128)(4,1)S(1)} %compare_and_fusion, bf16[128,2,16,128]{3,2,1,0:T(8,128)(2,1)} %bitcast.70, bf16[1024,2,128,1]{2,1,0,3:T(2,128)(2,1)} %bitcast.74), kind=kOutput, calls=%fused_computation.5 | convolution fusion | flops 1086320640 | bytes 18497536 | tf_op jit(solution)/shard_map/cond/branch_1_fun/rkgd,pkd->rkgp/dot_general | solution.py:51
  93.4 9.2 %convert_reduce_fusion = f32[128,2,16]{0,2,1:T(8,128)S(1)} fusion(f32[128,2,16]{0,2,1:T(8,128)S(1)} %broadcast_maximum_fusion, f32[2,1024,128,16]{2,1,3,0:T(8,128)} %get-tuple-element.49, pred[128,1024]{0,1:T(8,128)(4,1)S(1)} %compare_and_fusion), kind=kLoop, calls=%fused_computation.9 | loop fusion | flops 25161728 | bytes 16941056 | tf_op jit(solution)/shard_map/cond/branch_1_fun/reduce_sum | solution.py:68
  102.6 2.0 reshape.169
  104.6 12.1 %convolution_bitcast_fusion = f32[128,2,16,128]{3,0,2,1:T(8,128)} fusion(bf16[1024,2,128,1]{2,1,0,3:T(2,128)(2,1)} %bitcast.76, f32[2,1024,128,16]{2,1,3,0:T(8,128)} %get-tuple-element.49, f32[128,2,16]{0,2,1:T(8,128)S(1)} %broadcast_maximum_fusion, pred[128,1024]{0,1:T(8,128)(4,1)S(1)} %compare_and_fusion), kind=kOutput, calls=%fused_computation.10 | convolution fusion | flops 1090519040 | bytes 19546112 | tf_op jit(solution)/shard_map/cond/branch_1_fun/rkgp,pkd->rkgd/dot_general | solution.py:69
  116.7 3.0 copy.60
  119.7 2.9 divide_convert_fusion
  122.6 125.6 %all-gather.2.cloned.1.call-done = bf16[4096,2048]{1,0:T(8,128)(2,1)} async-done(((bf16[4096,256]{1,0:T(8,128)(2,1)}), bf16[4096,2048]{1,0:T(8,128)(2,1)}) %all-gather.2.cloned.1.call-update) | async-done | bytes 16777232 | tf_op jit(solution)/shard_map/all_gather | solution.py:106
  248.2 9.3 %convolution_convert_fusion.1 = bf16[128,2048]{1,0:T(8,128)(2,1)} fusion(bf16[128,4096]{0,1:T(8,128)(2,1)} %bitcast.69, bf16[4096,2048]{1,0:T(8,128)(2,1)} %all-gather.2.cloned.1.call-done), kind=kOutput, calls=%fused_computation.28 | convolution fusion | flops 2147745792 | bytes 18350080 | tf_op jit(solution)/shard_map/dot_general | solution.py:104
  257.5 0.0 reduce-scatter.2.cloned.1.call-update
  257.5 0.1 copy.49
  257.6 0.1 eq.42
  257.7 0.1 eq.46
  257.8 0.1 copy.48
  257.9 0.1 mul.66
  258.0 1.2 reduce-window.6
  259.1 0.2 slice_reduce_fusion
  259.4 0.1 fusion.29
  259.5 8.3 %reduce-scatter.2.cloned.1.call-done = bf16[64,2048]{1,0:T(8,128)(2,1)} async-done(((bf16[128,2048]{1,0:T(8,128)(2,1)}), bf16[64,2048]{1,0:T(8,128)(2,1)}) %reduce-scatter.2.cloned.1.call-update) | async-done | bytes 262160 | tf_op jit(solution)/shard_map/reduce_scatter | solution.py:109
  267.8 1.1 add_convert_fusion
  268.9 0.0 copy-start.3
  268.9 0.2 fusion.25
  269.0 0.8 fusion.27
  269.9 6.1 %scatter_custom_fusion = bf16[768,2048]{1,0:T(8,128)(2,1)} fusion(s32[512]{0:T(512)S(1)} %bitcast.77, bf16[]{:T(256)} %constant.60.clone.1, bf16[64,2048]{1,0:T(8,128)(2,1)} %fusion.27), kind=kCustom, calls=%fused_computation.30 | custom fusion | bytes 3407874 | tf_op jit(solution)/shard_map/scatter | solution.py:126
  276.0 75.8 %all_to_all.10 = bf16[16,48,2048]{2,1,0:T(8,128)(2,1)S(1)} all-to-all(bf16[16,48,2048]{2,1,0:T(8,128)(2,1)} %bitcast.68), channel_id=1, replica_groups=mesh['groups'=2,'sect'=8,'head'=2] {'sect','head'}, dimensions={0} | all-to-all | bytes 6291456 | tf_op jit(solution)/shard_map/all_to_all | solution.py:129
  351.8 1.7 copy-done.2
  353.5 4.0 fusion.13
  357.5 11.0 %convolution_convert_fusion = bf16[768,2048]{1,0:T(8,128)(2,1)} fusion(bf16[1,768,2048]{2,1,0:T(8,128)(2,1)S(1)} %copy-done, f32[768,768]{1,0:T(8,128)} %fusion.13, bf16[768,2048]{1,0:T(8,128)(2,1)} %bitcast.73, bf16[1,2048,768]{2,1,0:T(8,128)(2,1)} %param.23), kind=kOutput, calls=%fused_computation.22 | convolution fusion | flops 4836950016 | bytes 14942208 | tf_op jit(solution)/shard_map/dot_general | solution.py:134
  368.5 5.2 %all-to-all-start.1 = ((bf16[16,48,2048]{2,1,0:T(8,128)(2,1)}), bf16[16,48,2048]{2,1,0:T(8,128)(2,1)}, u32[]{:S(2)}, u32[]{:S(2)}) async-start(bf16[16,48,2048]{2,1,0:T(8,128)(2,1)} %bitcast.71), calls=%async_computation.2 | async-start | bytes 6291456 | tf_op jit(solution)/shard_map/all_to_all | solution.py:138
  373.8 0.1 copy.47
  373.9 69.9 %all-to-all-done.1 = bf16[16,48,2048]{2,1,0:T(8,128)(2,1)} async-done(((bf16[16,48,2048]{2,1,0:T(8,128)(2,1)}), bf16[16,48,2048]{2,1,0:T(8,128)(2,1)}, u32[]{:S(2)}, u32[]{:S(2)}) %all-to-all-start.1) | async-done | bytes 3145760 | tf_op jit(solution)/shard_map/all_to_all | solution.py:138
  443.7 7.6 %gather_fusion.1 = bf16[512,2048]{1,0:T(8,128)(2,1)} fusion(bf16[768,2048]{1,0:T(8,128)(2,1)} %bitcast.16, s32[1024]{0:T(1024)S(1)} %pad_clamp_fusion), kind=kCustom, calls=%fused_computation.1 | custom fusion | bytes 4196352 | tf_op jit(solution)/shard_map/gather | solution.py:142
  451.3 4.1 fusion.11
  (30 shorter events, 0.2 us)
Async XLA Ops:
  7.2 350.4 %copy-start = (bf16[1,768,2048]{2,1,0:T(8,128)(2,1)S(1)}, bf16[1,768,2048]{2,1,0:T(8,128)(2,1)}, u32[]{:S(2)}) copy-start(bf16[1,768,2048]{2,1,0:T(8,128)(2,1)} %param.25) | copy-start | bytes 9437188
  7.2 71.7 %copy-start.1 = (s32[1024]{0:T(1024)S(1)}, s32[1024]{0:T(1024)}, u32[]{:S(2)}) copy-start(s32[1024]{0:T(1024)} %param.17) | copy-start | bytes 12292
  7.2 38.2 %copy-start.4 = (bf16[128,256]{1,0:T(8,128)(2,1)S(1)}, bf16[128,256]{1,0:T(8,128)(2,1)}, u32[]{:S(2)}) copy-start(bf16[128,256]{1,0:T(8,128)(2,1)} %param.16) | copy-start | bytes 196612
  7.2 241.0 %all-gather.2.cloned.1.call-start = ((), (), s32[]{:S(2)}) async-start(), calls=%async_computation.3 | async-start | bytes 18874368 | tf_op jit(solution)/shard_map/all_gather | solution.py:106
  7.9 259.8 %reduce-scatter.2.cloned.1.call-start = ((), (), s32[]{:S(2)}) async-start(), calls=%async_computation.4 | async-start | bytes 786432 | tf_op jit(solution)/shard_map/reduce_scatter | solution.py:109
  248.2 9.3 %copy-start.5 = (s32[64,8]{0,1:T(8,128)S(1)}, s32[64,8]{0,1:T(8,128)}, u32[]{:S(2)}) copy-start(s32[64,8]{0,1:T(8,128)} %param.21) | copy-start | bytes 6148
  248.2 11.2 %copy-start.7 = (bf16[2048]{0:T(1024)(128)(2,1)S(1)}, bf16[2048]{0:T(1024)(128)(2,1)}, u32[]{:S(2)}) copy-start(bf16[2048]{0:T(1024)(128)(2,1)} %param.20) | copy-start | bytes 12292
  268.9 82.9 %copy-start.3 = (bf16[64,2048]{1,0:T(8,128)(2,1)}, bf16[64,2048]{1,0:T(8,128)(2,1)S(1)}, u32[]{:S(2)}) copy-start(bf16[64,2048]{1,0:T(8,128)(2,1)S(1)} %add_convert_fusion) | copy-start | bytes 786436
  276.0 77.5 %copy-start.8 = (bf16[1,2048,768]{2,1,0:T(8,128)(2,1)S(1)}, bf16[1,2048,768]{2,1,0:T(8,128)(2,1)}, u32[]{:S(2)}) copy-start(bf16[1,2048,768]{2,1,0:T(8,128)(2,1)} %param.24) | copy-start | bytes 9437188
  351.8 1.7 copy-start.2
  368.5 5.2 %copy-start.6 = (f32[64,8]{0,1:T(8,128)S(1)}, f32[64,8]{0,1:T(8,128)}, u32[]{:S(2)}) copy-start(f32[64,8]{0,1:T(8,128)} %param.22) | copy-start | bytes 6148
  368.5 75.2 %all-to-all-start.1 = ((bf16[16,48,2048]{2,1,0:T(8,128)(2,1)}), bf16[16,48,2048]{2,1,0:T(8,128)(2,1)}, u32[]{:S(2)}, u32[]{:S(2)}) async-start(bf16[16,48,2048]{2,1,0:T(8,128)(2,1)} %bitcast.71), calls=%async_computation.2 | async-start | bytes 6291456 | tf_op jit(solution)/shard_map/all_to_all | solution.py:138
Sparse Core Ops, SparseCore 0:
  10.1 238.0 all-gather.1
  257.6 10.1 reduce-scatter.1
where the time goes:
time: 463 us; the launch traced here: 462 us
  waiting for transfers between devices  204 us (44%)
  blocking collectives  141 us (30%)
  matrix products  46.1 us (10%)
  local copies, waits for them, and re-layouts  27.3 us (6%)
  other arithmetic  22.3 us (5%)
  between operations  15.5 us (3%)
  starting transfers between devices  5.31 us (1%)
    all_gather x1, waiting for transfers between devices, shards(): lax.all_gather(proj_weight, 'sect', axis=1, tiled=True)  126 us
    all_to_all x1, blocking collectives, shards(): lax.all_to_all(parcels, ('sect', 'head'), split_axis=0, concat_axis=0, ti...  75.8 us
    all_to_all x1, waiting for transfers between devices, shards(): lax.all_to_all(processed, ('sect', 'head'), split_axis=0, concat_axis=0,...  69.9 us
    all_gather x1, blocking collectives, attend(): value_piece = lax.all_gather(values, 'sect', axis=0, tiled=True)  33.5 us
    all_gather x1, blocking collectives, attend(): key_piece = lax.all_gather(packed_key_rows, 'sect', axis=0, tiled=True)  32.1 us
    dot_general x1, matrix products, compute(): jnp.einsum('rkgp,pkd->rkgd', weights, value_tensor_three, preferred_eleme...  12.1 us
    dot_general x1, matrix products, shards(): jnp.dot(hidden, down_weight[0], preferred_element_type=jnp.float32)  11 us
    dot_general x1, matrix products, compute(): jnp.einsum('rkgd,pkd->rkgp', query_tensor_four, key_tensor_three, preferr...  9.76 us
  transfers between devices with their start and end apart: 3, of which 3 were waited for; matrix products, arithmetic and copies ran while one was open for 11% of the time, Pallas kernels for 0%

commit v1 on v0

--- a/solution.py
+++ b/solution.py
@@ -32,8 +32,11 @@
         )
     running = tuple(initial_state)
     first_row = jnp.int32(0)
-    key_piece = lax.all_gather(packed_key_rows, "sect", axis=0, tiled=True)
-    value_piece = lax.all_gather(values, "sect", axis=0, tiled=True)
+    key_piece, value_piece = jnp.split(
+        lax.all_gather(jnp.concatenate([packed_key_rows, values], 1), "sect", axis=0, tiled=True),
+        [packed_key_rows.shape[1]],
+        1,
+    )
     piece_len = key_piece.shape[0]
     key_tensor_three = key_piece.reshape(piece_len, kv_heads, head_size)
     value_tensor_three = value_piece.reshape(piece_len, kv_heads, head_size)

time: 463 us -> 491 us (1.060)
  waiting for transfers between devices: 204 us -> 300 us
  blocking collectives: 141 us -> 75.8 us
    all_gather x2 -> x0, blocking collectives: 65.6 us -> none  [the longest x1 33.5 us: attend(): value_piece = lax.all_gather(values, 'sect', axis=0, tiled=True)]
    all_gather x1, waiting for transfers between devices: 126 us -> 187 us  [shards(): lax.all_gather(proj_weight, 'sect', axis=1, tiled=True)]
    all_gather x0 -> x1, waiting for transfers between devices: none -> 33.7 us  [attend(): lax.all_gather(jnp.concatenate([packed_key_rows, values], 1), 'sect', axi...]
  transfers between devices with their start and end apart: 3 -> 4, of which waited for: 3 -> 4; matrix products, arithmetic and copies ran while one was open for 11% -> 9% of each run, Pallas kernels for 0% -> 0%
where the time goes in v1:
time: 491 us; the launch traced here: 490 us
  waiting for transfers between devices  300 us (61%)
  blocking collectives  75.8 us (15%)
  matrix products  43.8 us (9%)
  local copies, waits for them, and re-layouts  26.3 us (5%)
  other arithmetic  23.6 us (5%)
  between operations  15.2 us (3%)
  starting transfers between devices  5.35 us (1%)
    all_gather x1, waiting for transfers between devices, shards(): lax.all_gather(proj_weight, 'sect', axis=1, tiled=True)  187 us
    all_to_all x1, blocking collectives, shards(): lax.all_to_all(parcels, ('sect', 'head'), split_axis=0, concat_axis=0, ti...  75.8 us
    all_to_all x1, waiting for transfers between devices, shards(): lax.all_to_all(processed, ('sect', 'head'), split_axis=0, concat_axis=0,...  69.9 us
    all_gather x1, waiting for transfers between devices, attend(): lax.all_gather(jnp.concatenate([packed_key_rows, values], 1), 'sect', axi...  33.7 us
    dot_general x1, matrix products, compute(): jnp.einsum('rkgp,pkd->rkgd', weights, value_tensor_three, preferred_eleme...  12 us
    dot_general x1, matrix products, shards(): jnp.dot(hidden, down_weight[0], preferred_element_type=jnp.float32)  11 us
    reduce_sum x1, other arithmetic, compute(): new_sum = jnp.sum(weights.astype(jnp.float32), axis=-1)  10.6 us
  transfers between devices with their start and end apart: 4, of which 4 were waited for; matrix products, arithmetic and copies ran while one was open for 9% of the time, Pallas kernels for 0%

profile of v1, /device:TPU:13, one launch (start us, length us, event | category | flops | bytes accessed | tf_op | source)
XLA Modules:
  0.0 490.1 jit_solution(7620530907223635590)
XLA Ops:
  7.2 0.0 copy-start
  7.2 0.0 all-gather.3.cloned.1.call-start
  7.2 1.1 copy.49
  8.3 1.0 copy.48
  9.3 0.7 pad_maximum_fusion
  10.0 0.0 all-gather.3.cloned.1.call-update
  10.0 0.0 all-gather.5.cloned.1.call-start
  10.1 0.7 all-gather.5.cloned.1.call-update
  10.8 0.0 reduce-scatter.2.cloned.1.call-start
  10.8 1.6 gather_fusion
  12.5 0.6 and_select_fusion.1
  13.8 0.2 convert_reduce_fusion.1
  14.0 0.6 reduce_min.9
  15.3 33.7 %all-gather.3.cloned.1.call-done = bf16[1024,512]{0,1:T(8,128)(2,1)} async-done(((bf16[128,512]{0,1:T(8,128)(2,1)}), bf16[1024,512]{0,1:T(8,128)(2,1)}) %all-gather.3.cloned.1.call-update) | async-done | bytes 1048592 | tf_op jit(solution)/shard_map/all_gather | solution.py:36
  49.0 36.9 %conditional.1 = (f32[128,2,16]{0,2,1:T(8,128)S(1)}, f32[128,2,16,128]{0,3,2,1:T(8,128)}) conditional(s32[]{:T(128)} %convert_element_type.61, () %tuple.16, (s32[1024]{0:T(1024)S(1)}, s32[128]{0:T(128)S(1)}, s32[128]{0:T(128)S(1)}, s32[128]{0:T(128)S(1)}, s32[1024]{0:T(1024)S(1)}, /*index=5*/s32[128]{0:T(128)S(1)}, bf16[1024,512]{0,1:T(8,128)(2,1)}, ...), branch_computations={%region_3.4_spmd, %region_4.0_spmd} | conditional | flops 2202399232 | bytes 63548432 | solution.py:77
  49.0 0.3 compare_and_fusion
  49.4 2.1 fusion.32
  51.4 1.5 copy.65
  52.9 7.5 %fusion = (f32[128,2,16]{0,2,1:T(8,128)S(1)}, f32[2,1024,128,16]{2,1,3,0:T(8,128)}) fusion(pred[128,1024]{0,1:T(8,128)(4,1)S(1)} %compare_and_fusion, bf16[1024,2,128,1]{0,2,3,1:T(8,128)(2,1)S(1)} %bitcast.84, bf16[128,2,16,128]{3,2,1,0:T(8,128)(2,1)S(1)} %bitcast.80), kind=kOutput, calls=%fused_computation.5 | convolution fusion | flops 1086320640 | bytes 18497536 | tf_op jit(solution)/shard_map/cond/branch_1_fun/rkgd,pkd->rkgp/dot_general | solution.py:54
  60.4 10.6 %convert_reduce_fusion = f32[128,2,16]{0,2,1:T(8,128)S(1)} fusion(f32[128,2,16]{0,2,1:T(8,128)S(1)} %broadcast_maximum_fusion, f32[2,1024,128,16]{2,1,3,0:T(8,128)} %get-tuple-element.51, pred[128,1024]{0,1:T(8,128)(4,1)S(1)} %compare_and_fusion), kind=kLoop, calls=%fused_computation.9 | loop fusion | flops 25161728 | bytes 16941056 | tf_op jit(solution)/shard_map/cond/branch_1_fun/reduce_sum | solution.py:71
  71.0 12.0 %convolution_bitcast_fusion = f32[128,2,16,128]{3,0,2,1:T(8,128)} fusion(bf16[1024,2,128,1]{0,2,3,1:T(8,128)(2,1)} %bitcast.86, f32[2,1024,128,16]{2,1,3,0:T(8,128)} %get-tuple-element.51, f32[128,2,16]{0,2,1:T(8,128)S(1)} %broadcast_maximum_fusion, pred[128,1024]{0,1:T(8,128)(4,1)S(1)} %compare_and_fusion), kind=kOutput, calls=%fused_computation.10 | convolution fusion | flops 1090519040 | bytes 19546112 | tf_op jit(solution)/shard_map/cond/branch_1_fun/rkgp,pkd->rkgd/dot_general | solution.py:72
  83.0 2.9 copy.64
  86.0 2.9 divide_convert_fusion
  88.8 187.5 %all-gather.5.cloned.1.call-done = bf16[4096,2048]{1,0:T(8,128)(2,1)} async-done(((bf16[4096,256]{1,0:T(8,128)(2,1)}), bf16[4096,2048]{1,0:T(8,128)(2,1)}) %all-gather.5.cloned.1.call-update) | async-done | bytes 16777232 | tf_op jit(solution)/shard_map/all_gather | solution.py:109
  276.3 9.3 %convolution_convert_fusion.1 = bf16[128,2048]{1,0:T(8,128)(2,1)} fusion(bf16[128,4096]{0,1:T(8,128)(2,1)} %bitcast.79, bf16[4096,2048]{1,0:T(8,128)(2,1)} %all-gather.5.cloned.1.call-done), kind=kOutput, calls=%fused_computation.26 | convolution fusion | flops 2147745792 | bytes 18350080 | tf_op jit(solution)/shard_map/dot_general | solution.py:107
  285.6 0.0 reduce-scatter.2.cloned.1.call-update
  285.6 0.1 copy.53
  285.7 0.1 eq.42
  285.8 0.1 eq.46
  285.9 0.1 copy.52
  286.0 0.1 mul.66
  286.1 1.2 reduce-window.6
  287.2 0.2 slice_reduce_fusion
  287.5 0.1 fusion.27
  287.6 8.3 %reduce-scatter.2.cloned.1.call-done = bf16[64,2048]{1,0:T(8,128)(2,1)} async-done(((bf16[128,2048]{1,0:T(8,128)(2,1)}), bf16[64,2048]{1,0:T(8,128)(2,1)}) %reduce-scatter.2.cloned.1.call-update) | async-done | bytes 262160 | tf_op jit(solution)/shard_map/reduce_scatter | solution.py:112
  295.9 1.1 add_convert_fusion
  297.0 0.2 fusion.23
  297.2 0.8 fusion.25
  298.0 6.1 %scatter_custom_fusion = bf16[768,2048]{1,0:T(8,128)(2,1)} fusion(s32[512]{0:T(512)S(1)} %bitcast.87, bf16[]{:T(256)} %constant.60.clone.1, bf16[64,2048]{1,0:T(8,128)(2,1)} %fusion.25), kind=kCustom, calls=%fused_computation.28 | custom fusion | bytes 3407874 | tf_op jit(solution)/shard_map/scatter | solution.py:129
  304.1 75.8 %all_to_all.10 = bf16[16,48,2048]{2,1,0:T(8,128)(2,1)S(1)} all-to-all(bf16[16,48,2048]{2,1,0:T(8,128)(2,1)} %bitcast.78), channel_id=1, replica_groups=mesh['groups'=2,'sect'=8,'head'=2] {'sect','head'}, dimensions={0} | all-to-all | bytes 6291456 | tf_op jit(solution)/shard_map/all_to_all | solution.py:132
  379.9 1.7 copy-done.2
  381.6 4.0 fusion.11
  385.6 11.0 %convolution_convert_fusion = bf16[768,2048]{1,0:T(8,128)(2,1)} fusion(bf16[1,768,2048]{2,1,0:T(8,128)(2,1)S(1)} %copy-done, f32[768,768]{1,0:T(8,128)} %fusion.11, bf16[768,2048]{1,0:T(8,128)(2,1)} %bitcast.83, bf16[1,2048,768]{2,1,0:T(8,128)(2,1)} %param.23), kind=kOutput, calls=%fused_computation.20 | convolution fusion | flops 4836950016 | bytes 14942208 | tf_op jit(solution)/shard_map/dot_general | solution.py:137
  396.6 5.2 %all-to-all-start.1 = ((bf16[16,48,2048]{2,1,0:T(8,128)(2,1)}), bf16[16,48,2048]{2,1,0:T(8,128)(2,1)}, u32[]{:S(2)}, u32[]{:S(2)}) async-start(bf16[16,48,2048]{2,1,0:T(8,128)(2,1)} %bitcast.81), calls=%async_computation.2 | async-start | bytes 6291456 | tf_op jit(solution)/shard_map/all_to_all | solution.py:141
  401.9 0.1 copy.51
  402.0 69.9 %all-to-all-done.1 = bf16[16,48,2048]{2,1,0:T(8,128)(2,1)} async-done(((bf16[16,48,2048]{2,1,0:T(8,128)(2,1)}), bf16[16,48,2048]{2,1,0:T(8,128)(2,1)}, u32[]{:S(2)}, u32[]{:S(2)}) %all-to-all-start.1) | async-done | bytes 3145760 | tf_op jit(solution)/shard_map/all_to_all | solution.py:141
  471.9 7.6 %gather_fusion.1 = bf16[512,2048]{1,0:T(8,128)(2,1)} fusion(bf16[768,2048]{1,0:T(8,128)(2,1)} %bitcast.18, s32[1024]{0:T(1024)S(1)} %pad_clamp_fusion), kind=kCustom, calls=%fused_computation.1 | custom fusion | bytes 4196352 | tf_op jit(solution)/shard_map/gather | solution.py:145
  479.4 4.1 fusion.9
  (31 shorter events, 0.2 us)
Async XLA Ops:
  7.2 378.5 %copy-start = (bf16[1,768,2048]{2,1,0:T(8,128)(2,1)S(1)}, bf16[1,768,2048]{2,1,0:T(8,128)(2,1)}, u32[]{:S(2)}) copy-start(bf16[1,768,2048]{2,1,0:T(8,128)(2,1)} %param.25) | copy-start | bytes 9437188
  7.2 6.6 %copy-start.1 = (s32[1024]{0:T(1024)S(1)}, s32[1024]{0:T(1024)}, u32[]{:S(2)}) copy-start(s32[1024]{0:T(1024)} %param.17) | copy-start | bytes 12292
  7.2 41.8 %all-gather.3.cloned.1.call-start = ((), (), s32[]{:S(2)}) async-start(), calls=%async_computation.3 | async-start | bytes 1179648 | tf_op jit(solution)/shard_map/all_gather | solution.py:36
  10.0 266.3 %all-gather.5.cloned.1.call-start = ((), (), s32[]{:S(2)}) async-start(), calls=%async_computation.4 | async-start | bytes 18874368 | tf_op jit(solution)/shard_map/all_gather | solution.py:109
  10.8 285.1 %reduce-scatter.2.cloned.1.call-start = ((), (), s32[]{:S(2)}) async-start(), calls=%async_computation.5 | async-start | bytes 786432 | tf_op jit(solution)/shard_map/reduce_scatter | solution.py:112
  276.3 9.3 %copy-start.4 = (s32[64,8]{0,1:T(8,128)S(1)}, s32[64,8]{0,1:T(8,128)}, u32[]{:S(2)}) copy-start(s32[64,8]{0,1:T(8,128)} %param.21) | copy-start | bytes 6148
  276.3 11.2 %copy-start.6 = (bf16[2048]{0:T(1024)(128)(2,1)S(1)}, bf16[2048]{0:T(1024)(128)(2,1)}, u32[]{:S(2)}) copy-start(bf16[2048]{0:T(1024)(128)(2,1)} %param.20) | copy-start | bytes 12292
  297.0 82.9 %copy-start.3 = (bf16[64,2048]{1,0:T(8,128)(2,1)}, bf16[64,2048]{1,0:T(8,128)(2,1)S(1)}, u32[]{:S(2)}) copy-start(bf16[64,2048]{1,0:T(8,128)(2,1)S(1)} %add_convert_fusion) | copy-start | bytes 786436
  304.1 77.5 %copy-start.7 = (bf16[1,2048,768]{2,1,0:T(8,128)(2,1)S(1)}, bf16[1,2048,768]{2,1,0:T(8,128)(2,1)}, u32[]{:S(2)}) copy-start(bf16[1,2048,768]{2,1,0:T(8,128)(2,1)} %param.24) | copy-start | bytes 9437188
  379.9 1.7 copy-start.2
  396.6 5.2 %copy-start.5 = (f32[64,8]{0,1:T(8,128)S(1)}, f32[64,8]{0,1:T(8,128)}, u32[]{:S(2)}) copy-start(f32[64,8]{0,1:T(8,128)} %param.22) | copy-start | bytes 6148
  396.6 75.2 %all-to-all-start.1 = ((bf16[16,48,2048]{2,1,0:T(8,128)(2,1)}), bf16[16,48,2048]{2,1,0:T(8,128)(2,1)}, u32[]{:S(2)}, u32[]{:S(2)}) async-start(bf16[16,48,2048]{2,1,0:T(8,128)(2,1)} %bitcast.81), calls=%async_computation.2 | async-start | bytes 6291456 | tf_op jit(solution)/shard_map/all_to_all | solution.py:141
Sparse Core Ops, SparseCore 0:
  10.6 38.3 all-gather.2
  51.0 225.1 all-gather.4
  285.7 10.1 reduce-scatter.1
